TPU v7x, 512 devices: a whole 4x4x16 slice. The times are simulated.
512 devices in a mesh: gx: 16 (over z), gy: 32 (over y, x, core).
Axes of the slice: x: 4, y: 4, z: 16, core: 2. Of those that a mesh axis runs over, the one named last changes fastest.
Arguments:
- initial_temp: float32 [1, 8192, 8192], P(None, 'gy', 'gx'), may hold values from -8 to 8
- kx_low: float32 [1, 8192, 8192], P(None, 'gy', 'gx'), may hold values from 6e-06 to 2000000
- ky_low: float32 [1, 8192, 8192], P(None, 'gy', 'gx'), may hold values from 6e-06 to 2000000
Outputs:
- new_temp: float32 [1, 8192, 8192], P(None, 'gy', 'gx')
All inputs are finite; a program needn't handle non-finite values.
Results may differ from a plain program's by a relative error of at most 0.00002.
Values sent between devices are 32-bit elements; how exact they have to be, the bound alone decides.
A program may use at most 64 MiB of HBM per device.

v0:
```python
import functools

import jax
import jax.numpy as jnp
from jax import lax
from jax.experimental import pallas as pl
from jax.experimental.pallas import tpu as pltpu
from jax.sharding import PartitionSpec as P

MESH = pl.DeviceIdType.MESH
SUB = 8
LANES = 128
WAYS = 4
REACH = 4
SHORT = 1e30


def recip(value):
    return pltpu.reciprocal(value, full_range=False)


def join_matrix(low, high):
    excess = low[1] + high[2]
    inverse = recip(excess + (low[0] + high[0]))
    to_low = low[0] * inverse
    to_high = high[0] * inverse
    joined = (to_low * high[0], high[1] + to_high * excess, low[2] + to_low * excess)
    return joined, (inverse, to_low, to_high)


def join_source(low, high, coefs):
    inverse, to_low, to_high = coefs
    source = low[0] + high[1]
    return (high[0] + to_high * source, low[1] + to_low * source), source * inverse


def next_rows(value, steps):
    return pltpu.roll(value, SUB - steps, 1)


def tree_matrix(blocks, coef_ref, lanes):
    def keep(slot, coefs):
        for place, coef in enumerate(coefs):
            coef_ref[3 * slot + place, lanes] = coef

    first, coefs = join_matrix(blocks[0], blocks[1])
    keep(0, coefs)
    second, coefs = join_matrix(blocks[2], blocks[3])
    keep(1, coefs)
    joined, coefs = join_matrix(first, second)
    keep(2, coefs)
    for level in range(3):
        other = tuple(next_rows(member, 1 << level) for member in joined)
        joined, coefs = join_matrix(joined, other)
        keep(3 + level, coefs)
    return joined


def tree_source(blocks, coef_ref, mid_ref, lanes):
    def coefs(slot):
        return tuple(coef_ref[3 * slot + place, lanes] for place in range(3))

    first, mid = join_source(blocks[0], blocks[1], coefs(0))
    mid_ref[0, lanes] = mid
    second, mid = join_source(blocks[2], blocks[3], coefs(1))
    mid_ref[1, lanes] = mid
    joined, mid = join_source(first, second, coefs(2))
    mid_ref[2, lanes] = mid
    for level in range(3):
        other = tuple(next_rows(member, 1 << level) for member in joined)
        joined, mid = join_source(joined, other, coefs(3 + level))
        mid_ref[3 + level, lanes] = mid
    return joined


def spread(value, level, row):
    for bit in range(level + 1):
        value = jnp.where((row & (1 << bit)) != 0, pltpu.roll(value, 1 << bit, 1), value)
    return value


def spread_coefs(coef_ref, lanes, row):
    for level in range(3):
        for place in (1, 2):
            slot = 3 * (3 + level) + place
            coef_ref[slot, lanes] = spread(coef_ref[slot, lanes], level, row)


def spread_mids(mid_ref, lanes, row):
    for level in range(3):
        mid_ref[3 + level, lanes] = spread(mid_ref[3 + level, lanes], level, row)


def tree_down(left, right, coef_ref, mid_ref, lanes, row):
    def middle(slot, low, high):
        return (
            mid_ref[slot, lanes]
            + coef_ref[3 * slot + 1, lanes] * low
            + coef_ref[3 * slot + 2, lanes] * high
        )

    for level in (2, 1, 0):
        mid = middle(3 + level, left, right)
        lower = (row & (1 << level)) == 0
        left, right = jnp.where(lower, left, mid), jnp.where(lower, mid, right)
    center = middle(2, left, right)
    lower_mid = middle(0, left, center)
    upper_mid = middle(1, center, right)
    return (left, lower_mid, center, upper_mid, right)


def solve_pair(own_matrix, own_source, rest_matrix, rest_source):
    link = own_matrix[0] + rest_matrix[0]
    own_excess = own_matrix[1] + rest_matrix[2]
    prev_excess = own_matrix[2] + rest_matrix[1]
    own_total = own_source[0] + rest_source[1]
    prev_total = own_source[1] + rest_source[0]
    inverse = recip(own_excess * prev_excess + link * (own_excess + prev_excess))
    both = link * (own_total + prev_total)
    own_value = (own_total * prev_excess + both) * inverse
    prev_value = (prev_total * own_excess + both) * inverse
    return own_value, prev_value


def kernel(
    count_x,
    count_y,
    temp_hbm,
    kx_hbm,
    ky_hbm,
    out_hbm,
    temp_ref,
    kx_ref,
    ky_ref,
    temp_turned,
    kx_turned,
    half_ref,
    x_link,
    x_next,
    x_mid,
    y_link,
    y_next,
    y_inverse,
    y_mid,
    x_coefs,
    x_mids,
    y_coefs,
    y_mids,
    ring_coefs,
    ring_mids,
    x_send,
    x_pair_send,
    x_recv,
    x_pair_recv,
    y_matrix_send,
    y_matrix_recv,
    y_source_send,
    y_source_recv,
    in_sems,
    out_sems,
    x_send_sems,
    x_recv_sems,
    pair_send_sems,
    pair_recv_sems,
    matrix_send_sems,
    matrix_recv_sems,
    source_send_sems,
    source_recv_sems,
):
    rows, columns = temp_ref.shape
    blocks_x = rows // LANES
    blocks_y = columns // LANES
    my_x = lax.axis_index("gx")
    my_y = lax.axis_index("gy")
    loads = [
        pltpu.make_async_copy(kx_hbm, kx_ref, in_sems.at[0]),
        pltpu.make_async_copy(temp_hbm, temp_ref, in_sems.at[1]),
    ] + [
        pltpu.make_async_copy(
            ky_hbm.at[:, pl.ds(LANES * block, LANES)], ky_ref.at[block], in_sems.at[2 + block]
        )
        for block in range(blocks_y)
    ]
    for load in loads:
        load.start()

    def peer_x(offset):
        return {"gx": lax.rem(my_x + (offset + count_x), count_x)}

    def peer_y(offset):
        return {"gy": lax.rem(my_y + offset, count_y)}

    offsets = [sign * step for step in range(REACH, 0, -1) for sign in (1, -1)]
    barrier = pltpu.get_barrier_semaphore()
    for offset in offsets:
        pl.semaphore_signal(barrier, inc=1, device_id=peer_x(offset), device_id_type=MESH)
    for offset in range(1, count_y):
        pl.semaphore_signal(barrier, inc=1, device_id=peer_y(offset), device_id_type=MESH)

    def slot_of(offset):
        return offset + REACH - (1 if offset > 0 else 0)

    shape_x = (blocks_x, SUB, LANES)
    row_x = lax.broadcasted_iota(jnp.int32, shape_x, 1)
    every = slice(0, blocks_x)
    length_x = columns // (WAYS * SUB)
    length_y = rows // (WAYS * SUB)

    def rows_of(way, step, length):
        return pl.ds(way * length + step, SUB, stride=WAYS * length)

    def turn_in(source, target):
        for block in range(blocks_x):
            for left in range(0, columns, LANES):
                target[block, left : left + LANES, :] = source[
                    LANES * block : LANES * (block + 1), left : left + LANES
                ].T

    loads[0].wait()
    turn_in(kx_ref, kx_turned)
    loads[1].wait()
    turn_in(temp_ref, temp_turned)

    excess = [jnp.ones(shape_x, jnp.float32)] * WAYS
    link = [kx_turned[:, rows_of(way, 0, length_x), :] for way in range(WAYS)]
    source = [temp_turned[:, rows_of(way, 0, length_x), :] for way in range(WAYS)]
    left_excess = [jnp.zeros(shape_x, jnp.float32)] * WAYS
    left_source = [jnp.zeros(shape_x, jnp.float32)] * WAYS
    for step in range(length_x - 1):
        for way in range(WAYS):
            face = kx_turned[:, rows_of(way, step + 1, length_x), :]
            inverse = recip(excess[way] + link[way] + face)
            to_next = face * inverse
            to_left = link[way] * inverse
            x_next[step, way] = to_next
            x_link[step, way] = to_left
            x_mid[step, way] = source[way] * inverse
            left_excess[way] = left_excess[way] + to_left * excess[way]
            left_source[way] = left_source[way] + to_left * source[way]
            link[way] = to_left * face
            excess[way] = 1.0 + to_next * excess[way]
            source[way] = (
                temp_turned[:, rows_of(way, step + 1, length_x), :] + to_next * source[way]
            )
    matrix = [(link[way], excess[way], left_excess[way]) for way in range(WAYS)]
    own_matrix = tree_matrix(matrix, x_coefs, every)
    own_source = tree_source(
        [(source[way], left_source[way]) for way in range(WAYS)], x_coefs, x_mids, every
    )
    for place, member in enumerate(own_matrix + own_source):
        x_send[:, place : place + 1, :] = member[:, 0:1, :]

    pl.semaphore_wait(barrier, len(offsets) + count_y - 1)

    x_copies = {}
    for offset in offsets:
        x_copies[offset] = pltpu.make_async_remote_copy(
            src_ref=x_send,
            dst_ref=x_recv.at[slot_of(-offset)],
            send_sem=x_send_sems.at[slot_of(offset)],
            recv_sem=x_recv_sems.at[slot_of(-offset)],
            device_id=peer_x(offset),
            device_id_type=MESH,
        )
        x_copies[offset].start()

    for load in loads[2:]:
        load.wait()
    width = 2
    shape_y = (width, SUB, LANES)
    groups = [slice(start, start + width) for start in range(0, blocks_y, width)]
    row_y = lax.broadcasted_iota(jnp.int32, shape_y, 1)
    for lanes in groups:
        excess = [jnp.ones(shape_y, jnp.float32)] * WAYS
        link = [ky_ref[lanes, rows_of(way, 0, length_y), :] for way in range(WAYS)]
        left_excess = [jnp.zeros(shape_y, jnp.float32)] * WAYS
        for step in range(length_y - 1):
            for way in range(WAYS):
                face = ky_ref[lanes, rows_of(way, step + 1, length_y), :]
                inverse = recip(excess[way] + link[way] + face)
                to_next = face * inverse
                to_left = link[way] * inverse
                y_next[step, way, lanes] = to_next
                y_link[step, way, lanes] = to_left
                y_inverse[step, way, lanes] = inverse
                left_excess[way] = left_excess[way] + to_left * excess[way]
                link[way] = to_left * face
                excess[way] = 1.0 + to_next * excess[way]
        matrix = [(link[way], excess[way], left_excess[way]) for way in range(WAYS)]
        joined = tree_matrix(matrix, y_coefs, lanes)
        for place, member in enumerate(joined):
            y_matrix_send[lanes, place : place + 1, :] = member[:, 0:1, :]

    def to_y_peers(source, target, send_sems, recv_sems):
        height = source.shape[1]
        copies = []
        for offset in range(1, count_y):
            slot = count_y - 1 - offset
            copies.append(
                pltpu.make_async_remote_copy(
                    src_ref=source,
                    dst_ref=target.at[:, pl.ds(SUB * slot, height), :],
                    send_sem=send_sems.at[slot],
                    recv_sem=recv_sems.at[slot],
                    device_id=peer_y(offset),
                    device_id_type=MESH,
                )
            )
            copies[-1].start()
        return copies

    matrix_copies = to_y_peers(y_matrix_send, y_matrix_recv, matrix_send_sems, matrix_recv_sems)

    spare = SUB * (count_y - 1)
    y_matrix_recv[:, spare : spare + 1, :] = jnp.full((blocks_y, 1, LANES), SHORT, jnp.float32)
    y_matrix_recv[:, spare + 1 : spare + 3, :] = jnp.zeros((blocks_y, 2, LANES), jnp.float32)
    y_source_recv[:, spare : spare + 2, :] = jnp.zeros((blocks_y, 2, LANES), jnp.float32)
    spread_coefs(x_coefs, every, row_x)
    spread_mids(x_mids, every, row_x)

    def load_block(ref):
        return (
            tuple(ref[:, place : place + 1, :] for place in range(3)),
            tuple(ref[:, place : place + 1, :] for place in range(3, 5)),
        )

    def join(low, high):
        matrix, coefs = join_matrix(low[0], high[0])
        source, _ = join_source(low[1], high[1], coefs)
        return matrix, source

    for offset in offsets:
        x_copies[-offset].wait_recv()
    near = {offset: load_block(x_recv.at[slot_of(offset)]) for offset in offsets}
    above = join(join(near[1], near[2]), join(near[3], near[4]))
    below_three = join(near[-3], join(near[-2], near[-1]))
    below = join(near[-4], below_three)
    pair_copies = []
    for place, (block, offset) in enumerate(((above, -REACH), (below_three, REACH))):
        for index, member in enumerate(block[0] + block[1]):
            x_pair_send[place, :, index : index + 1, :] = member
        pair_copies.append(
            pltpu.make_async_remote_copy(
                src_ref=x_pair_send.at[place],
                dst_ref=x_pair_recv.at[place],
                send_sem=pair_send_sems.at[place],
                recv_sem=pair_recv_sems.at[place],
                device_id=peer_x(offset),
                device_id_type=MESH,
            )
        )
        pair_copies[-1].start()

    for copy in matrix_copies:
        copy.wait_recv()
    rings = []
    for lanes in groups:
        blocks = [
            tuple(
                y_matrix_recv[lanes, pl.ds(SUB * way + place, SUB, stride=WAYS * SUB), :]
                for place in range(3)
            )
            for way in range(WAYS)
        ]
        rings.append(tree_matrix(blocks, ring_coefs, lanes))

    for copy in pair_copies:
        copy.wait_recv()
    far_above = load_block(x_pair_recv.at[0])
    far_below = load_block(x_pair_recv.at[1])
    rest = join(join(above, far_above), join(far_below, below))
    own = load_block(x_send)
    own_value, prev_value = solve_pair(own[0], own[1], rest[0], rest[1])

    nodes = tree_down(
        jnp.broadcast_to(prev_value, shape_x),
        jnp.broadcast_to(own_value, shape_x),
        x_coefs,
        x_mids,
        every,
        row_x,
    )
    values = list(nodes[1:])
    for way in range(WAYS):
        temp_turned[:, rows_of(way, length_x - 1, length_x), :] = values[way]
    for step in range(length_x - 2, -1, -1):
        for way in range(WAYS):
            values[way] = (x_mid[step, way] + x_link[step, way] * nodes[way]) + x_next[
                step, way
            ] * values[way]
            temp_turned[:, rows_of(way, step, length_x), :] = values[way]
    for block in range(blocks_x):
        for other in range(blocks_y):
            half_ref[other, LANES * block : LANES * (block + 1), :] = temp_turned[
                block, LANES * other : LANES * (other + 1), :
            ].T

    for lanes in groups:
        source = [half_ref[lanes, rows_of(way, 0, length_y), :] for way in range(WAYS)]
        left_source = [jnp.zeros(shape_y, jnp.float32)] * WAYS
        for step in range(length_y - 1):
            for way in range(WAYS):
                y_mid[step, way, lanes] = source[way] * y_inverse[step, way, lanes]
                left_source[way] = left_source[way] + y_link[step, way, lanes] * source[way]
                source[way] = (
                    half_ref[lanes, rows_of(way, step + 1, length_y), :]
                    + y_next[step, way, lanes] * source[way]
                )
        joined = tree_source(
            [(source[way], left_source[way]) for way in range(WAYS)], y_coefs, y_mids, lanes
        )
        for place, member in enumerate(joined):
            y_source_send[lanes, place : place + 1, :] = member[:, 0:1, :]
    source_copies = to_y_peers(y_source_send, y_source_recv, source_send_sems, source_recv_sems)
    for lanes in groups:
        spread_coefs(y_coefs, lanes, row_y)
        spread_mids(y_mids, lanes, row_y)
    for copy in source_copies:
        copy.wait_recv()

    stores = []
    for group, lanes in enumerate(groups):
        blocks = [
            tuple(
                y_source_recv[lanes, pl.ds(SUB * way + place, SUB, stride=WAYS * SUB), :]
                for place in range(2)
            )
            for way in range(WAYS)
        ]
        ring_source = tree_source(blocks, ring_coefs, ring_mids, lanes)
        own_value, prev_value = solve_pair(
            tuple(y_matrix_send[lanes, place : place + 1, :] for place in range(3)),
            tuple(y_source_send[lanes, place : place + 1, :] for place in range(2)),
            tuple(member[:, 0:1, :] for member in rings[group]),
            tuple(member[:, 0:1, :] for member in ring_source),
        )
        nodes = tree_down(
            jnp.broadcast_to(prev_value, shape_y),
            jnp.broadcast_to(own_value, shape_y),
            y_coefs,
            y_mids,
            lanes,
            row_y,
        )
        values = list(nodes[1:])
        for way in range(WAYS):
            half_ref[lanes, rows_of(way, length_y - 1, length_y), :] = values[way]
        for step in range(length_y - 2, -1, -1):
            for way in range(WAYS):
                values[way] = (
                    y_mid[step, way, lanes] + y_link[step, way, lanes] * nodes[way]
                ) + y_next[step, way, lanes] * values[way]
                half_ref[lanes, rows_of(way, step, length_y), :] = values[way]
        for block in range(lanes.start, lanes.stop):
            stores.append(
                pltpu.make_async_copy(
                    half_ref.at[block],
                    out_hbm.at[:, pl.ds(LANES * block, LANES)],
                    out_sems.at[block],
                )
            )
            stores[-1].start()

    for copy in x_copies.values():
        copy.wait_send()
    for copy in pair_copies + matrix_copies + source_copies:
        copy.wait_send()
    for store in stores:
        store.wait()


def body(initial_temp, kx_low, ky_low):
    count_x = lax.axis_size("gx")
    count_y = lax.axis_size("gy")
    _, rows, columns = initial_temp.shape
    length_x = columns // (WAYS * SUB)
    length_y = rows // (WAYS * SUB)
    blocks_x = rows // LANES
    blocks_y = columns // LANES

    def vmem(*shape):
        return pltpu.VMEM(shape, jnp.float32)

    def sems(*shape):
        return pltpu.SemaphoreType.DMA(shape)

    result = pl.pallas_call(
        functools.partial(kernel, count_x, count_y),
        out_shape=jax.ShapeDtypeStruct((rows, columns), jnp.float32),
        in_specs=[pl.BlockSpec(memory_space=pl.ANY)] * 3,
        out_specs=pl.BlockSpec(memory_space=pl.ANY),
        scratch_shapes=[
            vmem(rows, columns),
            vmem(rows, columns),
            vmem(blocks_y, rows, LANES),
            vmem(blocks_x, columns, LANES),
            vmem(blocks_x, columns, LANES),
            vmem(blocks_y, rows, LANES),
            vmem(length_x - 1, WAYS, blocks_x, SUB, LANES),
            vmem(length_x - 1, WAYS, blocks_x, SUB, LANES),
            vmem(length_x - 1, WAYS, blocks_x, SUB, LANES),
            vmem(length_y - 1, WAYS, blocks_y, SUB, LANES),
            vmem(length_y - 1, WAYS, blocks_y, SUB, LANES),
            vmem(length_y - 1, WAYS, blocks_y, SUB, LANES),
            vmem(length_y - 1, WAYS, blocks_y, SUB, LANES),
            vmem(18, blocks_x, SUB, LANES),
            vmem(6, blocks_x, SUB, LANES),
            vmem(18, blocks_y, SUB, LANES),
            vmem(6, blocks_y, SUB, LANES),
            vmem(18, blocks_y, SUB, LANES),
            vmem(6, blocks_y, SUB, LANES),
            vmem(blocks_x, 5, LANES),
            vmem(2, blocks_x, 5, LANES),
            vmem(2 * REACH, blocks_x, 5, LANES),
            vmem(2, blocks_x, 5, LANES),
            vmem(blocks_y, 3, LANES),
            vmem(blocks_y, count_y * SUB, LANES),
            vmem(blocks_y, 2, LANES),
            vmem(blocks_y, count_y * SUB, LANES),
            sems(2 + blocks_y),
            sems(blocks_y),
            sems(2 * REACH),
            sems(2 * REACH),
            sems(2),
            sems(2),
            sems(count_y - 1),
            sems(count_y - 1),
            sems(count_y - 1),
            sems(count_y - 1),
        ],
        compiler_params=pltpu.CompilerParams(collective_id=0, has_side_effects=True),
    )(initial_temp[0], kx_low[0], ky_low[0])
    return result[None]


def solution(mesh):
    spec = P(None, "gy", "gx")
    return jax.shard_map(
        body, mesh=mesh, in_specs=(spec, spec, spec), out_specs=spec, check_vma=False
    )
```

profile of v0, /device:TPU:1, one launch (start us, length us, event | category | flops | bytes accessed | tf_op | source)
XLA Modules:
  0.0 34.7 jit_solution(13849660877338985756)
XLA Ops:
  0.0 32.8 %shard_map.37 = f32[256,512]{1,0:T(8,128)} custom-call(f32[256,512]{1,0:T(8,128)} %bitcast.5, f32[256,512]{1,0:T(8,128)} %bitcast.6, f32[256,512]{1,0:T(8,128)} %bitcast.7), custom_call_target="tpu_custom_call" | custom-call | tf_op jit(solution)/shard_map/pallas_call | solution.py:487
  32.8 1.9 %copy.5 = f32[1,256,512]{2,1,0:T(8,128)} copy(f32[1,256,512]{2,1,0:T(8,128)} %bitcast.4) | data formatting | bytes 1048576
where the time goes:
time: 34.9 us; the launch traced here: 34.7 us
  Pallas kernels  32.8 us (94%)
  local copies, waits for them, and re-layouts  1.87 us (5%)
    pallas_call x1, Pallas kernels, body(): pl.pallas_call(functools.partial(kernel, count_x, count_y), out_shape=jax...  32.8 us
    unnamed x1, local copies, waits for them, and re-layouts  1.87 us

commit v1 on v0

--- a/solution.py
+++ b/solution.py
@@ -13,6 +13,9 @@
 WAYS = 4
 REACH = 4
 SHORT = 1e30
+SLOT_RUN = 36
+ROOM = 24 * 1024 * 1024
+SMALL_ROOM = 1024 * 1024
 
 
 def recip(value):
@@ -93,11 +96,8 @@
 
 def tree_down(left, right, coef_ref, mid_ref, lanes, row):
     def middle(slot, low, high):
-        return (
-            mid_ref[slot, lanes]
-            + coef_ref[3 * slot + 1, lanes] * low
-            + coef_ref[3 * slot + 2, lanes] * high
-        )
+        value = coef_ref[3 * slot + 1, lanes] * low + coef_ref[3 * slot + 2, lanes] * high
+        return value if mid_ref is None else mid_ref[slot, lanes] + value
 
     for level in (2, 1, 0):
         mid = middle(3 + level, left, right)
@@ -128,13 +128,19 @@
     temp_hbm,
     kx_hbm,
     ky_hbm,
-    out_hbm,
+    out_ref,
     temp_ref,
     kx_ref,
+    ky_flat,
     ky_ref,
     temp_turned,
     kx_turned,
-    half_ref,
+    third_turned,
+    local_field,
+    left_field,
+    right_field,
+    own_column,
+    prev_column,
     x_link,
     x_next,
     x_mid,
@@ -157,7 +163,6 @@
     y_source_send,
     y_source_recv,
     in_sems,
-    out_sems,
     x_send_sems,
     x_recv_sems,
     pair_send_sems,
@@ -175,11 +180,7 @@
     loads = [
         pltpu.make_async_copy(kx_hbm, kx_ref, in_sems.at[0]),
         pltpu.make_async_copy(temp_hbm, temp_ref, in_sems.at[1]),
-    ] + [
-        pltpu.make_async_copy(
-            ky_hbm.at[:, pl.ds(LANES * block, LANES)], ky_ref.at[block], in_sems.at[2 + block]
-        )
-        for block in range(blocks_y)
+        pltpu.make_async_copy(ky_hbm, ky_flat, in_sems.at[2]),
     ]
     for load in loads:
         load.start()
@@ -207,14 +208,25 @@
     length_y = rows // (WAYS * SUB)
 
     def rows_of(way, step, length):
-        return pl.ds(way * length + step, SUB, stride=WAYS * length)
+        return pl.ds(way * length + step, SUB, stride=WAYS * length + 1)
+
+    def put(target, first, values, length):
+        run = WAYS * length
+        for top in range(0, values.shape[0], min(run, values.shape[0])):
+            place = first + top
+            target[pl.ds(place + place // run, min(run, values.shape[0])), :] = values[
+                top : top + min(run, values.shape[0])
+            ]
 
     def turn_in(source, target):
         for block in range(blocks_x):
             for left in range(0, columns, LANES):
-                target[block, left : left + LANES, :] = source[
-                    LANES * block : LANES * (block + 1), left : left + LANES
-                ].T
+                put(
+                    target.at[block],
+                    left,
+                    source[LANES * block : LANES * (block + 1), left : left + LANES].T,
+                    length_x,
+                )
 
     loads[0].wait()
     turn_in(kx_ref, kx_turned)
@@ -264,8 +276,9 @@
         )
         x_copies[offset].start()
 
-    for load in loads[2:]:
-        load.wait()
+    loads[2].wait()
+    for block in range(blocks_y):
+        put(ky_ref.at[block], 0, ky_flat[:, LANES * block : LANES * (block + 1)], length_y)
     width = 2
     shape_y = (width, SUB, LANES)
     groups = [slice(start, start + width) for start in range(0, blocks_y, width)]
@@ -291,6 +304,9 @@
         for place, member in enumerate(joined):
             y_matrix_send[lanes, place : place + 1, :] = member[:, 0:1, :]
 
+    def row_of_slot(slot):
+        return SLOT_RUN * (slot // WAYS) + SUB * (slot % WAYS)
+
     def to_y_peers(source, target, send_sems, recv_sems):
         height = source.shape[1]
         copies = []
@@ -299,7 +315,7 @@
             copies.append(
                 pltpu.make_async_remote_copy(
                     src_ref=source,
-                    dst_ref=target.at[:, pl.ds(SUB * slot, height), :],
+                    dst_ref=target.at[:, pl.ds(row_of_slot(slot), height), :],
                     send_sem=send_sems.at[slot],
                     recv_sem=recv_sems.at[slot],
                     device_id=peer_y(offset),
@@ -311,12 +327,37 @@
 
     matrix_copies = to_y_peers(y_matrix_send, y_matrix_recv, matrix_send_sems, matrix_recv_sems)
 
-    spare = SUB * (count_y - 1)
+    spare = row_of_slot(count_y - 1)
     y_matrix_recv[:, spare : spare + 1, :] = jnp.full((blocks_y, 1, LANES), SHORT, jnp.float32)
     y_matrix_recv[:, spare + 1 : spare + 3, :] = jnp.zeros((blocks_y, 2, LANES), jnp.float32)
     y_source_recv[:, spare : spare + 2, :] = jnp.zeros((blocks_y, 2, LANES), jnp.float32)
     spread_coefs(x_coefs, every, row_x)
     spread_mids(x_mids, every, row_x)
+
+    zeros = jnp.zeros(shape_x, jnp.float32)
+    ones = jnp.ones(shape_x, jnp.float32)
+    for left, right, mids, cells, turned, field in (
+        (zeros, zeros, x_mids, x_mid, temp_turned, local_field),
+        (ones, zeros, None, None, kx_turned, left_field),
+        (zeros, ones, None, None, third_turned, right_field),
+    ):
+        nodes = tree_down(left, right, x_coefs, mids, every, row_x)
+        values = list(nodes[1:])
+        for way in range(WAYS):
+            turned[:, rows_of(way, length_x - 1, length_x), :] = values[way]
+        for step in range(length_x - 2, -1, -1):
+            for way in range(WAYS):
+                value = x_link[step, way] * nodes[way] + x_next[step, way] * values[way]
+                values[way] = value if cells is None else cells[step, way] + value
+                turned[:, rows_of(way, step, length_x), :] = values[way]
+        for block in range(blocks_x):
+            for other in range(blocks_y):
+                run = WAYS * length_x
+                parts = [
+                    turned[block, pl.ds(place + place // run, run), :]
+                    for place in range(LANES * other, LANES * (other + 1), run)
+                ]
+                put(field.at[other], LANES * block, jnp.concatenate(parts, axis=0).T, length_y)
 
     def load_block(ref):
         return (
@@ -357,7 +398,7 @@
     for lanes in groups:
         blocks = [
             tuple(
-                y_matrix_recv[lanes, pl.ds(SUB * way + place, SUB, stride=WAYS * SUB), :]
+                y_matrix_recv[lanes, pl.ds(SUB * way + place, SUB, stride=SLOT_RUN), :]
                 for place in range(3)
             )
             for way in range(WAYS)
@@ -372,38 +413,27 @@
     own = load_block(x_send)
     own_value, prev_value = solve_pair(own[0], own[1], rest[0], rest[1])
 
-    nodes = tree_down(
-        jnp.broadcast_to(prev_value, shape_x),
-        jnp.broadcast_to(own_value, shape_x),
-        x_coefs,
-        x_mids,
-        every,
-        row_x,
-    )
-    values = list(nodes[1:])
-    for way in range(WAYS):
-        temp_turned[:, rows_of(way, length_x - 1, length_x), :] = values[way]
-    for step in range(length_x - 2, -1, -1):
-        for way in range(WAYS):
-            values[way] = (x_mid[step, way] + x_link[step, way] * nodes[way]) + x_next[
-                step, way
-            ] * values[way]
-            temp_turned[:, rows_of(way, step, length_x), :] = values[way]
-    for block in range(blocks_x):
-        for other in range(blocks_y):
-            half_ref[other, LANES * block : LANES * (block + 1), :] = temp_turned[
-                block, LANES * other : LANES * (other + 1), :
-            ].T
+    for value, column in ((own_value, own_column), (prev_value, prev_column)):
+        for block in range(blocks_x):
+            put(column, LANES * block, jnp.broadcast_to(value[block], (LANES, LANES)).T, length_y)
+
+    def half_rows(lanes, way, step):
+        rows_here = rows_of(way, step, length_y)
+        return (
+            local_field[lanes, rows_here, :]
+            + prev_column[rows_here, :] * left_field[lanes, rows_here, :]
+            + own_column[rows_here, :] * right_field[lanes, rows_here, :]
+        )
 
     for lanes in groups:
-        source = [half_ref[lanes, rows_of(way, 0, length_y), :] for way in range(WAYS)]
+        source = [half_rows(lanes, way, 0) for way in range(WAYS)]
         left_source = [jnp.zeros(shape_y, jnp.float32)] * WAYS
         for step in range(length_y - 1):
             for way in range(WAYS):
                 y_mid[step, way, lanes] = source[way] * y_inverse[step, way, lanes]
                 left_source[way] = left_source[way] + y_link[step, way, lanes] * source[way]
                 source[way] = (
-                    half_ref[lanes, rows_of(way, step + 1, length_y), :]
+                    half_rows(lanes, way, step + 1)
                     + y_next[step, way, lanes] * source[way]
                 )
         joined = tree_source(
@@ -418,11 +448,10 @@
     for copy in source_copies:
         copy.wait_recv()
 
-    stores = []
     for group, lanes in enumerate(groups):
         blocks = [
             tuple(
-                y_source_recv[lanes, pl.ds(SUB * way + place, SUB, stride=WAYS * SUB), :]
+                y_source_recv[lanes, pl.ds(SUB * way + place, SUB, stride=SLOT_RUN), :]
                 for place in range(2)
             )
             for way in range(WAYS)
@@ -444,27 +473,33 @@
         )
         values = list(nodes[1:])
         for way in range(WAYS):
-            half_ref[lanes, rows_of(way, length_y - 1, length_y), :] = values[way]
+            out_ref[lanes, rows_of(way, length_y - 1, length_y), :] = values[way]
         for step in range(length_y - 2, -1, -1):
             for way in range(WAYS):
                 values[way] = (
                     y_mid[step, way, lanes] + y_link[step, way, lanes] * nodes[way]
                 ) + y_next[step, way, lanes] * values[way]
-                half_ref[lanes, rows_of(way, step, length_y), :] = values[way]
-        for block in range(lanes.start, lanes.stop):
-            stores.append(
-                pltpu.make_async_copy(
-                    half_ref.at[block],
-                    out_hbm.at[:, pl.ds(LANES * block, LANES)],
-                    out_sems.at[block],
-                )
-            )
-            stores[-1].start()
+                out_ref[lanes, rows_of(way, step, length_y), :] = values[way]
 
     for copy in x_copies.values():
         copy.wait_send()
     for copy in pair_copies + matrix_copies + source_copies:
         copy.wait_send()
+
+
+def put_out(blocks_ref, out_hbm, sems):
+    run = out_hbm.shape[0] // SUB
+    stores = [
+        pltpu.make_async_copy(
+            blocks_ref.at[block, pl.ds((run + 1) * part, run)],
+            out_hbm.at[pl.ds(run * part, run), pl.ds(LANES * block, LANES)],
+            sems.at[block, part],
+        )
+        for block in range(blocks_ref.shape[0])
+        for part in range(SUB)
+    ]
+    for store in stores:
+        store.start()
     for store in stores:
         store.wait()
 
@@ -484,18 +519,24 @@
     def sems(*shape):
         return pltpu.SemaphoreType.DMA(shape)
 
-    result = pl.pallas_call(
+    blocks = pl.pallas_call(
         functools.partial(kernel, count_x, count_y),
-        out_shape=jax.ShapeDtypeStruct((rows, columns), jnp.float32),
-        in_specs=[pl.BlockSpec(memory_space=pl.ANY)] * 3,
-        out_specs=pl.BlockSpec(memory_space=pl.ANY),
+        out_shape=jax.ShapeDtypeStruct((blocks_y, rows + SUB, LANES), jnp.float32),
+        in_specs=[pl.BlockSpec(memory_space=pltpu.HBM)] * 3,
+        out_specs=pl.BlockSpec(memory_space=pltpu.VMEM),
         scratch_shapes=[
             vmem(rows, columns),
             vmem(rows, columns),
-            vmem(blocks_y, rows, LANES),
-            vmem(blocks_x, columns, LANES),
-            vmem(blocks_x, columns, LANES),
-            vmem(blocks_y, rows, LANES),
+            vmem(rows, columns),
+            vmem(blocks_y, rows + SUB, LANES),
+            vmem(blocks_x, columns + SUB, LANES),
+            vmem(blocks_x, columns + SUB, LANES),
+            vmem(blocks_x, columns + SUB, LANES),
+            vmem(blocks_y, rows + SUB, LANES),
+            vmem(blocks_y, rows + SUB, LANES),
+            vmem(blocks_y, rows + SUB, LANES),
+            vmem(rows + SUB, LANES),
+            vmem(rows + SUB, LANES),
             vmem(length_x - 1, WAYS, blocks_x, SUB, LANES),
             vmem(length_x - 1, WAYS, blocks_x, SUB, LANES),
             vmem(length_x - 1, WAYS, blocks_x, SUB, LANES),
@@ -514,11 +555,10 @@
             vmem(2 * REACH, blocks_x, 5, LANES),
             vmem(2, blocks_x, 5, LANES),
             vmem(blocks_y, 3, LANES),
-            vmem(blocks_y, count_y * SUB, LANES),
+            vmem(blocks_y, SUB * SLOT_RUN, LANES),
             vmem(blocks_y, 2, LANES),
-            vmem(blocks_y, count_y * SUB, LANES),
-            sems(2 + blocks_y),
-            sems(blocks_y),
+            vmem(blocks_y, SUB * SLOT_RUN, LANES),
+            sems(3),
             sems(2 * REACH),
             sems(2 * REACH),
             sems(2),
@@ -528,8 +568,18 @@
             sems(count_y - 1),
             sems(count_y - 1),
         ],
-        compiler_params=pltpu.CompilerParams(collective_id=0, has_side_effects=True),
-    )(initial_temp[0], kx_low[0], ky_low[0])
+        compiler_params=pltpu.CompilerParams(
+            collective_id=0, has_side_effects=True, vmem_limit_bytes=ROOM
+        ),
+    )(*(pltpu.with_memory_space_constraint(value[0], pltpu.HBM) for value in (initial_temp, kx_low, ky_low)))
+    result = pl.pallas_call(
+        put_out,
+        out_shape=jax.ShapeDtypeStruct((rows, columns), jnp.float32),
+        in_specs=[pl.BlockSpec(memory_space=pltpu.VMEM)],
+        out_specs=pl.BlockSpec(memory_space=pltpu.HBM),
+        scratch_shapes=[sems(blocks_y, SUB)],
+        compiler_params=pltpu.CompilerParams(vmem_limit_bytes=SMALL_ROOM),
+    )(blocks)
     return result[None]
 
 

time: 34.9 us -> 32.5 us (0.931)
  local copies, waits for them, and re-layouts: 1.87 us -> 0 us
  Pallas kernels: 32.8 us -> 32.3 us
    unnamed x1 -> x0, local copies, waits for them, and re-layouts: 1.87 us -> none
    pallas_call x1, Pallas kernels: 32.8 us -> 31.3 us  [body(): pl.pallas_call(functools.partial(kernel, count_x, count_y), out_shape=jax...]
    pallas_call x0 -> x1, Pallas kernels: none -> 1.06 us  [body(): pl.pallas_call(put_out, out_shape=jax.ShapeDtypeStruct((rows, columns), j...]
where the time goes in v1:
time: 32.5 us; the launch traced here: 32.3 us
  Pallas kernels  32.3 us (99%)
    pallas_call x1, Pallas kernels, body(): pl.pallas_call(functools.partial(kernel, count_x, count_y), out_shape=jax...  31.3 us
    pallas_call x1, Pallas kernels, body(): pl.pallas_call(put_out, out_shape=jax.ShapeDtypeStruct((rows, columns), j...  1.06 us

profile of v1, /device:TPU:1, one launch (start us, length us, event | category | flops | bytes accessed | tf_op | source)
XLA Modules:
  0.0 32.3 jit_solution(16607889934966651183)
XLA Ops:
  0.0 31.3 %shard_map.37.blocks_ref = f32[4,264,128]{2,1,0:T(8,128)S(1)} custom-call(f32[256,512]{1,0:T(8,128)} %bitcast.4, f32[256,512]{1,0:T(8,128)} %bitcast.5, f32[256,512]{1,0:T(8,128)} %bitcast.6), custom_call_target="tpu_custom_call" | custom-call | tf_op jit(solution)/shard_map/pallas_call | solution.py:522
  31.3 1.1 %shard_map.38 = f32[256,512]{1,0:T(8,128)} custom-call(f32[4,264,128]{2,1,0:T(8,128)S(1)} %shard_map.37.blocks_ref), custom_call_target="tpu_custom_call" | custom-call | tf_op jit(solution)/shard_map/pallas_call | solution.py:575

commit v2 on v1

--- a/solution.py
+++ b/solution.py
@@ -13,6 +13,7 @@
 WAYS = 4
 REACH = 4
 SHORT = 1e30
+RING = 4
 SLOT_RUN = 36
 ROOM = 24 * 1024 * 1024
 SMALL_ROOM = 1024 * 1024
@@ -163,14 +164,14 @@
     y_source_send,
     y_source_recv,
     in_sems,
-    x_send_sems,
-    x_recv_sems,
-    pair_send_sems,
-    pair_recv_sems,
-    matrix_send_sems,
-    matrix_recv_sems,
-    source_send_sems,
-    source_recv_sems,
+    x_send_sem,
+    x_recv_sem,
+    pair_send_sem,
+    pair_recv_sem,
+    matrix_send_sem,
+    matrix_recv_sem,
+    source_send_sem,
+    source_recv_sem,
 ):
     rows, columns = temp_ref.shape
     blocks_x = rows // LANES
@@ -192,11 +193,25 @@
         return {"gy": lax.rem(my_y + offset, count_y)}
 
     offsets = [sign * step for step in range(REACH, 0, -1) for sign in (1, -1)]
+
+    def hops_y(offset):
+        ring = offset // 2 // RING % RING
+        place = offset // 2 % RING
+        return min(ring, RING - ring) + min(place, RING - place)
+
+    offsets_y = sorted(range(1, count_y), key=lambda offset: -hops_y(offset))
     barrier = pltpu.get_barrier_semaphore()
-    for offset in offsets:
-        pl.semaphore_signal(barrier, inc=1, device_id=peer_x(offset), device_id_type=MESH)
-    for offset in range(1, count_y):
-        pl.semaphore_signal(barrier, inc=1, device_id=peer_y(offset), device_id_type=MESH)
+    for steps in range(REACH, -1, -1):
+        for offset in offsets:
+            if abs(offset) == steps:
+                pl.semaphore_signal(
+                    barrier, inc=1, device_id=peer_x(offset), device_id_type=MESH
+                )
+        for offset in offsets_y:
+            if min(REACH, hops_y(offset)) == steps:
+                pl.semaphore_signal(
+                    barrier, inc=1, device_id=peer_y(offset), device_id_type=MESH
+                )
 
     def slot_of(offset):
         return offset + REACH - (1 if offset > 0 else 0)
@@ -264,17 +279,15 @@
 
     pl.semaphore_wait(barrier, len(offsets) + count_y - 1)
 
-    x_copies = {}
     for offset in offsets:
-        x_copies[offset] = pltpu.make_async_remote_copy(
+        pltpu.make_async_remote_copy(
             src_ref=x_send,
             dst_ref=x_recv.at[slot_of(-offset)],
-            send_sem=x_send_sems.at[slot_of(offset)],
-            recv_sem=x_recv_sems.at[slot_of(-offset)],
+            send_sem=x_send_sem,
+            recv_sem=x_recv_sem,
             device_id=peer_x(offset),
             device_id_type=MESH,
-        )
-        x_copies[offset].start()
+        ).start()
 
     loads[2].wait()
     for block in range(blocks_y):
@@ -307,25 +320,23 @@
     def row_of_slot(slot):
         return SLOT_RUN * (slot // WAYS) + SUB * (slot % WAYS)
 
-    def to_y_peers(source, target, send_sems, recv_sems):
+    def to_y_peers(source, target, send_sem, recv_sem):
         height = source.shape[1]
-        copies = []
-        for offset in range(1, count_y):
+        for offset in offsets_y:
             slot = count_y - 1 - offset
-            copies.append(
-                pltpu.make_async_remote_copy(
-                    src_ref=source,
-                    dst_ref=target.at[:, pl.ds(row_of_slot(slot), height), :],
-                    send_sem=send_sems.at[slot],
-                    recv_sem=recv_sems.at[slot],
-                    device_id=peer_y(offset),
-                    device_id_type=MESH,
-                )
-            )
-            copies[-1].start()
-        return copies
-
-    matrix_copies = to_y_peers(y_matrix_send, y_matrix_recv, matrix_send_sems, matrix_recv_sems)
+            pltpu.make_async_remote_copy(
+                src_ref=source,
+                dst_ref=target.at[:, pl.ds(row_of_slot(slot), height), :],
+                send_sem=send_sem,
+                recv_sem=recv_sem,
+                device_id=peer_y(offset),
+                device_id_type=MESH,
+            ).start()
+
+    def all_peers(target, source):
+        return target.at[:, pl.ds(0, source.shape[1] * (count_y - 1)), :]
+
+    to_y_peers(y_matrix_send, y_matrix_recv, matrix_send_sem, matrix_recv_sem)
 
     spare = row_of_slot(count_y - 1)
     y_matrix_recv[:, spare : spare + 1, :] = jnp.full((blocks_y, 1, LANES), SHORT, jnp.float32)
@@ -370,30 +381,24 @@
         source, _ = join_source(low[1], high[1], coefs)
         return matrix, source
 
-    for offset in offsets:
-        x_copies[-offset].wait_recv()
+    await_bytes(x_recv, x_recv_sem)
     near = {offset: load_block(x_recv.at[slot_of(offset)]) for offset in offsets}
     above = join(join(near[1], near[2]), join(near[3], near[4]))
     below_three = join(near[-3], join(near[-2], near[-1]))
     below = join(near[-4], below_three)
-    pair_copies = []
     for place, (block, offset) in enumerate(((above, -REACH), (below_three, REACH))):
         for index, member in enumerate(block[0] + block[1]):
             x_pair_send[place, :, index : index + 1, :] = member
-        pair_copies.append(
-            pltpu.make_async_remote_copy(
-                src_ref=x_pair_send.at[place],
-                dst_ref=x_pair_recv.at[place],
-                send_sem=pair_send_sems.at[place],
-                recv_sem=pair_recv_sems.at[place],
-                device_id=peer_x(offset),
-                device_id_type=MESH,
-            )
-        )
-        pair_copies[-1].start()
-
-    for copy in matrix_copies:
-        copy.wait_recv()
+        pltpu.make_async_remote_copy(
+            src_ref=x_pair_send.at[place],
+            dst_ref=x_pair_recv.at[place],
+            send_sem=pair_send_sem,
+            recv_sem=pair_recv_sem,
+            device_id=peer_x(offset),
+            device_id_type=MESH,
+        ).start()
+
+    await_bytes(all_peers(y_matrix_recv, y_matrix_send), matrix_recv_sem)
     rings = []
     for lanes in groups:
         blocks = [
@@ -405,8 +410,7 @@
         ]
         rings.append(tree_matrix(blocks, ring_coefs, lanes))
 
-    for copy in pair_copies:
-        copy.wait_recv()
+    await_bytes(x_pair_recv, pair_recv_sem)
     far_above = load_block(x_pair_recv.at[0])
     far_below = load_block(x_pair_recv.at[1])
     rest = join(join(above, far_above), join(far_below, below))
@@ -441,12 +445,11 @@
         )
         for place, member in enumerate(joined):
             y_source_send[lanes, place : place + 1, :] = member[:, 0:1, :]
-    source_copies = to_y_peers(y_source_send, y_source_recv, source_send_sems, source_recv_sems)
+    to_y_peers(y_source_send, y_source_recv, source_send_sem, source_recv_sem)
     for lanes in groups:
         spread_coefs(y_coefs, lanes, row_y)
         spread_mids(y_mids, lanes, row_y)
-    for copy in source_copies:
-        copy.wait_recv()
+    await_bytes(all_peers(y_source_recv, y_source_send), source_recv_sem)
 
     for group, lanes in enumerate(groups):
         blocks = [
@@ -481,27 +484,30 @@
                 ) + y_next[step, way, lanes] * values[way]
                 out_ref[lanes, rows_of(way, step, length_y), :] = values[way]
 
-    for copy in x_copies.values():
-        copy.wait_send()
-    for copy in pair_copies + matrix_copies + source_copies:
-        copy.wait_send()
-
-
-def put_out(blocks_ref, out_hbm, sems):
+    await_bytes(x_recv, x_send_sem)
+    await_bytes(x_pair_recv, pair_send_sem)
+    await_bytes(all_peers(y_matrix_recv, y_matrix_send), matrix_send_sem)
+    await_bytes(all_peers(y_source_recv, y_source_send), source_send_sem)
+
+
+def await_bytes(ref, sem):
+    pltpu.make_async_copy(ref, ref, sem).wait()
+
+
+def put_out(blocks_ref, out_hbm, sem):
     run = out_hbm.shape[0] // SUB
     stores = [
         pltpu.make_async_copy(
             blocks_ref.at[block, pl.ds((run + 1) * part, run)],
             out_hbm.at[pl.ds(run * part, run), pl.ds(LANES * block, LANES)],
-            sems.at[block, part],
+            sem,
         )
         for block in range(blocks_ref.shape[0])
         for part in range(SUB)
     ]
     for store in stores:
         store.start()
-    for store in stores:
-        store.wait()
+    await_bytes(out_hbm, sem)
 
 
 def body(initial_temp, kx_low, ky_low):
@@ -550,24 +556,17 @@
             vmem(6, blocks_y, SUB, LANES),
             vmem(18, blocks_y, SUB, LANES),
             vmem(6, blocks_y, SUB, LANES),
-            vmem(blocks_x, 5, LANES),
-            vmem(2, blocks_x, 5, LANES),
-            vmem(2 * REACH, blocks_x, 5, LANES),
-            vmem(2, blocks_x, 5, LANES),
+            vmem(blocks_x, SUB, LANES),
+            vmem(2, blocks_x, SUB, LANES),
+            vmem(2 * REACH, blocks_x, SUB, LANES),
+            vmem(2, blocks_x, SUB, LANES),
             vmem(blocks_y, 3, LANES),
             vmem(blocks_y, SUB * SLOT_RUN, LANES),
             vmem(blocks_y, 2, LANES),
             vmem(blocks_y, SUB * SLOT_RUN, LANES),
             sems(3),
-            sems(2 * REACH),
-            sems(2 * REACH),
-            sems(2),
-            sems(2),
-            sems(count_y - 1),
-            sems(count_y - 1),
-            sems(count_y - 1),
-            sems(count_y - 1),
-        ],
+        ]
+        + [pltpu.SemaphoreType.DMA] * 8,
         compiler_params=pltpu.CompilerParams(
             collective_id=0, has_side_effects=True, vmem_limit_bytes=ROOM
         ),
@@ -577,7 +576,7 @@
         out_shape=jax.ShapeDtypeStruct((rows, columns), jnp.float32),
         in_specs=[pl.BlockSpec(memory_space=pltpu.VMEM)],
         out_specs=pl.BlockSpec(memory_space=pltpu.HBM),
-        scratch_shapes=[sems(blocks_y, SUB)],
+        scratch_shapes=[pltpu.SemaphoreType.DMA],
         compiler_params=pltpu.CompilerParams(vmem_limit_bytes=SMALL_ROOM),
     )(blocks)
     return result[None]

time: 32.5 us -> 30.9 us (0.951)
  Pallas kernels: 32.3 us -> 30.8 us
    pallas_call x1, Pallas kernels: 31.3 us -> 30 us  [body(): pl.pallas_call(functools.partial(kernel, count_x, count_y), out_shape=jax...]
where the time goes in v2:
time: 30.9 us; the launch traced here: 30.8 us
  Pallas kernels  30.8 us (100%)
    pallas_call x1, Pallas kernels, body(): pl.pallas_call(functools.partial(kernel, count_x, count_y), out_shape=jax...  30 us
    pallas_call x1, Pallas kernels, body(): pl.pallas_call(put_out, out_shape=jax.ShapeDtypeStruct((rows, columns), j...  0.78 us

profile of v2, /device:TPU:1, one launch (start us, length us, event | category | flops | bytes accessed | tf_op | source)
XLA Modules:
  0.0 30.8 jit_solution(1679688264495842416)
XLA Ops:
  0.0 30.0 %shard_map.37.blocks_ref = f32[4,264,128]{2,1,0:T(8,128)S(1)} custom-call(f32[256,512]{1,0:T(8,128)} %bitcast.4, f32[256,512]{1,0:T(8,128)} %bitcast.5, f32[256,512]{1,0:T(8,128)} %bitcast.6), custom_call_target="tpu_custom_call" | custom-call | tf_op jit(solution)/shard_map/pallas_call | solution.py:528
  30.0 0.8 %shard_map.38 = f32[256,512]{1,0:T(8,128)} custom-call(f32[4,264,128]{2,1,0:T(8,128)S(1)} %shard_map.37.blocks_ref), custom_call_target="tpu_custom_call" | custom-call | tf_op jit(solution)/shard_map/pallas_call | solution.py:574

commit v3 on v2

--- a/solution.py
+++ b/solution.py
@@ -172,6 +172,8 @@
     matrix_recv_sem,
     source_send_sem,
     source_recv_sem,
+    rings_sem,
+    partner_sem,
 ):
     rows, columns = temp_ref.shape
     blocks_x = rows // LANES
@@ -201,17 +203,21 @@
 
     offsets_y = sorted(range(1, count_y), key=lambda offset: -hops_y(offset))
     barrier = pltpu.get_barrier_semaphore()
-    for steps in range(REACH, -1, -1):
-        for offset in offsets:
-            if abs(offset) == steps:
-                pl.semaphore_signal(
-                    barrier, inc=1, device_id=peer_x(offset), device_id_type=MESH
-                )
-        for offset in offsets_y:
-            if min(REACH, hops_y(offset)) == steps:
-                pl.semaphore_signal(
-                    barrier, inc=1, device_id=peer_y(offset), device_id_type=MESH
-                )
+    for offset in offsets:
+        pl.semaphore_signal(barrier, inc=1, device_id=peer_x(offset), device_id_type=MESH)
+
+    core = lax.rem(my_y, 2)
+    place = lax.rem(my_y // 2, RING)
+    ring = my_y // (2 * RING)
+
+    def at(ring, place, core):
+        return {"gy": (ring * RING + place) * 2 + core}
+
+    own_ring = [at(ring, lax.rem(place + step, RING), core) for step in (2, 1, 3)]
+    other_rings = [at(lax.rem(ring + step, RING), place, core) for step in (2, 1, 3)]
+    partner = at(ring, place, 1 - core)
+    for peer in own_ring + other_rings + [partner]:
+        pl.semaphore_signal(barrier, inc=1, device_id=peer, device_id_type=MESH)
 
     def slot_of(offset):
         return offset + REACH - (1 if offset > 0 else 0)
@@ -277,7 +283,7 @@
     for place, member in enumerate(own_matrix + own_source):
         x_send[:, place : place + 1, :] = member[:, 0:1, :]
 
-    pl.semaphore_wait(barrier, len(offsets) + count_y - 1)
+    pl.semaphore_wait(barrier, len(offsets) + len(own_ring) + len(other_rings) + 1)
 
     for offset in offsets:
         pltpu.make_async_remote_copy(
@@ -288,6 +294,9 @@
             device_id=peer_x(offset),
             device_id_type=MESH,
         ).start()
+
+    for peer in other_rings:
+        pl.semaphore_signal(rings_sem, inc=1, device_id=peer, device_id_type=MESH)
 
     loads[2].wait()
     for block in range(blocks_y):
@@ -336,7 +345,6 @@
     def all_peers(target, source):
         return target.at[:, pl.ds(0, source.shape[1] * (count_y - 1)), :]
 
-    to_y_peers(y_matrix_send, y_matrix_recv, matrix_send_sem, matrix_recv_sem)
 
     spare = row_of_slot(count_y - 1)
     y_matrix_recv[:, spare : spare + 1, :] = jnp.full((blocks_y, 1, LANES), SHORT, jnp.float32)
@@ -398,17 +406,10 @@
             device_id_type=MESH,
         ).start()
 
-    await_bytes(all_peers(y_matrix_recv, y_matrix_send), matrix_recv_sem)
-    rings = []
-    for lanes in groups:
-        blocks = [
-            tuple(
-                y_matrix_recv[lanes, pl.ds(SUB * way + place, SUB, stride=SLOT_RUN), :]
-                for place in range(3)
-            )
-            for way in range(WAYS)
-        ]
-        rings.append(tree_matrix(blocks, ring_coefs, lanes))
+    pl.semaphore_wait(rings_sem, len(other_rings))
+    pl.semaphore_signal(partner_sem, inc=1, device_id=partner, device_id_type=MESH)
+    pl.semaphore_wait(partner_sem, 1)
+    to_y_peers(y_matrix_send, y_matrix_recv, matrix_send_sem, matrix_recv_sem)
 
     await_bytes(x_pair_recv, pair_recv_sem)
     far_above = load_block(x_pair_recv.at[0])
@@ -449,6 +450,18 @@
     for lanes in groups:
         spread_coefs(y_coefs, lanes, row_y)
         spread_mids(y_mids, lanes, row_y)
+    await_bytes(all_peers(y_matrix_recv, y_matrix_send), matrix_recv_sem)
+    rings = []
+    for lanes in groups:
+        blocks = [
+            tuple(
+                y_matrix_recv[lanes, pl.ds(SUB * way + place, SUB, stride=SLOT_RUN), :]
+                for place in range(3)
+            )
+            for way in range(WAYS)
+        ]
+        rings.append(tree_matrix(blocks, ring_coefs, lanes))
+
     await_bytes(all_peers(y_source_recv, y_source_send), source_recv_sem)
 
     for group, lanes in enumerate(groups):
@@ -566,7 +579,8 @@
             vmem(blocks_y, SUB * SLOT_RUN, LANES),
             sems(3),
         ]
-        + [pltpu.SemaphoreType.DMA] * 8,
+        + [pltpu.SemaphoreType.DMA] * 8
+        + [pltpu.SemaphoreType.REGULAR] * 2,
         compiler_params=pltpu.CompilerParams(
             collective_id=0, has_side_effects=True, vmem_limit_bytes=ROOM
         ),

time: 30.9 us -> 30.8 us (level)
  no operation moved by 1% of the time
where the time goes in v3:
time: 30.8 us; the launch traced here: 30.7 us
  Pallas kernels  30.7 us (100%)
    pallas_call x1, Pallas kernels, body(): pl.pallas_call(functools.partial(kernel, count_x, count_y), out_shape=jax...  29.9 us
    pallas_call x1, Pallas kernels, body(): pl.pallas_call(put_out, out_shape=jax.ShapeDtypeStruct((rows, columns), j...  0.78 us

profile of v3, /device:TPU:1, one launch (start us, length us, event | category | flops | bytes accessed | tf_op | source)
XLA Modules:
  0.0 30.7 jit_solution(503276902188420714)
XLA Ops:
  0.0 29.9 %shard_map.37.blocks_ref = f32[4,264,128]{2,1,0:T(8,128)S(1)} custom-call(f32[256,512]{1,0:T(8,128)} %bitcast.4, f32[256,512]{1,0:T(8,128)} %bitcast.5, f32[256,512]{1,0:T(8,128)} %bitcast.6), custom_call_target="tpu_custom_call" | custom-call | tf_op jit(solution)/shard_map/pallas_call | solution.py:541
  29.9 0.8 %shard_map.38 = f32[256,512]{1,0:T(8,128)} custom-call(f32[4,264,128]{2,1,0:T(8,128)S(1)} %shard_map.37.blocks_ref), custom_call_target="tpu_custom_call" | custom-call | tf_op jit(solution)/shard_map/pallas_call | solution.py:588

commit v4 on v3

--- a/solution.py
+++ b/solution.py
@@ -165,7 +165,7 @@
     y_source_recv,
     in_sems,
     x_send_sem,
-    x_recv_sem,
+    x_recv_sems,
     pair_send_sem,
     pair_recv_sem,
     matrix_send_sem,
@@ -290,7 +290,7 @@
             src_ref=x_send,
             dst_ref=x_recv.at[slot_of(-offset)],
             send_sem=x_send_sem,
-            recv_sem=x_recv_sem,
+            recv_sem=x_recv_sems.at[1 if offset < 0 else 0],
             device_id=peer_x(offset),
             device_id_type=MESH,
         ).start()
@@ -389,12 +389,18 @@
         source, _ = join_source(low[1], high[1], coefs)
         return matrix, source
 
-    await_bytes(x_recv, x_recv_sem)
-    near = {offset: load_block(x_recv.at[slot_of(offset)]) for offset in offsets}
-    above = join(join(near[1], near[2]), join(near[3], near[4]))
-    below_three = join(near[-3], join(near[-2], near[-1]))
-    below = join(near[-4], below_three)
-    for place, (block, offset) in enumerate(((above, -REACH), (below_three, REACH))):
+    def near(offset):
+        return load_block(x_recv.at[slot_of(offset)])
+
+    for place, offset in ((0, -REACH), (1, REACH)):
+        side = 1 - place
+        await_bytes(x_recv.at[pl.ds(REACH * side, REACH)], x_recv_sems.at[side])
+        if side == 1:
+            above = join(join(near(1), near(2)), join(near(3), near(4)))
+            block = above
+        else:
+            below_three = join(near(-3), join(near(-2), near(-1)))
+            block = below_three
         for index, member in enumerate(block[0] + block[1]):
             x_pair_send[place, :, index : index + 1, :] = member
         pltpu.make_async_remote_copy(
@@ -405,6 +411,8 @@
             device_id=peer_x(offset),
             device_id_type=MESH,
         ).start()
+
+    below = join(near(-4), below_three)
 
     pl.semaphore_wait(rings_sem, len(other_rings))
     pl.semaphore_signal(partner_sem, inc=1, device_id=partner, device_id_type=MESH)
@@ -579,7 +587,8 @@
             vmem(blocks_y, SUB * SLOT_RUN, LANES),
             sems(3),
         ]
-        + [pltpu.SemaphoreType.DMA] * 8
+        + [pltpu.SemaphoreType.DMA, sems(2)]
+        + [pltpu.SemaphoreType.DMA] * 6
         + [pltpu.SemaphoreType.REGULAR] * 2,
         compiler_params=pltpu.CompilerParams(
             collective_id=0, has_side_effects=True, vmem_limit_bytes=ROOM

time: 30.8 us -> 30.8 us (level)
  no operation moved by 1% of the time
where the time goes in v4:
time: 30.8 us; the launch traced here: 30.7 us
  Pallas kernels  30.7 us (100%)
    pallas_call x1, Pallas kernels, body(): pl.pallas_call(functools.partial(kernel, count_x, count_y), out_shape=jax...  29.9 us
    pallas_call x1, Pallas kernels, body(): pl.pallas_call(put_out, out_shape=jax.ShapeDtypeStruct((rows, columns), j...  0.78 us

profile of v4, /device:TPU:1, one launch (start us, length us, event | category | flops | bytes accessed | tf_op | source)
XLA Modules:
  0.0 30.7 jit_solution(5315235127506560303)
XLA Ops:
  0.0 29.9 %shard_map.37.blocks_ref = f32[4,264,128]{2,1,0:T(8,128)S(1)} custom-call(f32[256,512]{1,0:T(8,128)} %bitcast.4, f32[256,512]{1,0:T(8,128)} %bitcast.5, f32[256,512]{1,0:T(8,128)} %bitcast.6), custom_call_target="tpu_custom_call" | custom-call | tf_op jit(solution)/shard_map/pallas_call | solution.py:549
  29.9 0.8 %shard_map.38 = f32[256,512]{1,0:T(8,128)} custom-call(f32[4,264,128]{2,1,0:T(8,128)S(1)} %shard_map.37.blocks_ref), custom_call_target="tpu_custom_call" | custom-call | tf_op jit(solution)/shard_map/pallas_call | solution.py:597
